TPU v7x, 32 devices: a whole 2x2x4 slice. The times are simulated.
32 devices in a mesh: dp: 8 (over z, x), seq: 4 (over y, core).
Axes of the slice: x: 2, y: 2, z: 4, core: 2. Of those that a mesh axis runs over, the one named last changes fastest.
Arguments:
- spatial_qkv: bfloat16 [8, 3, 4, 128, 1152], P('dp', None, 'seq'), may hold values from -24 to 24
- temporal_qkv: bfloat16 [8, 3, 4, 128, 1152], P('dp', None, 'seq'), may hold values from -24 to 24
- cotangent: bfloat16 [8, 4, 128, 1152], P('dp', 'seq'), may hold values from -6 to 6
- spatial_gate: float32 [8, 1152], P('dp'), may hold values from -4 to 4
- temporal_gate: float32 [8, 1152], P('dp'), may hold values from -4 to 4
- temporal_proj: bfloat16 [1152, 1152], replicated, may hold values from -0.1875 to 0.1875
- live_counts: int32 [8, 2], P('dp'), may hold values from 2 to 128, as said below
Outputs:
- temporal_qkv_grad: bfloat16 [8, 3, 4, 128, 1152], P('dp', None, 'seq')
- spatial_proj_grad: float32 [1152, 1152], P('seq', 'dp')
- temporal_proj_grad: float32 [1152, 1152], P('seq', 'dp')
Inputs may be any that keep to these rules, and one draw needn't show every extreme that they name: live_counts[g, 0] counts a clip's live frames, at most 4; live_counts[g, 1] counts the live positions of each of its frames, at most 128; in every draw some clip has all 4 frames and all 128 positions live.
All inputs are finite; a program needn't handle non-finite values.
Results may differ from a plain program's by a relative error of at most 0.015.
Values may be sent and summed in bfloat16 or wider, within the bound.
A program may use at most 64 MiB of HBM per device.

v0:
```python
import jax
import jax.numpy as jnp
from jax import lax
from jax.sharding import PartitionSpec as P

HEADS = 16
HD = 72


def attend(queries, key_block, value_block, key_keep, score_form, mix_form):
    head_split = queries.shape[:-1] + (HEADS, HD)
    q_heads = queries.reshape(head_split)
    k_heads = key_block.reshape(head_split)
    v_heads = value_block.reshape(head_split)
    scores = jnp.einsum(score_form, q_heads, k_heads, preferred_element_type=jnp.float32) * HD ** (
        -0.5
    )
    scores = jnp.where(key_keep[:, None, None, :], scores, -1e30)
    shifted = scores - jnp.max(scores, axis=-1, keepdims=True)
    expo = jnp.exp(shifted)
    attention_weights = (expo / jnp.sum(expo, axis=-1, keepdims=True)).astype(jnp.bfloat16)
    mixed = jnp.einsum(mix_form, attention_weights, v_heads, preferred_element_type=jnp.float32)
    return mixed.reshape(queries.shape)


def body(
    spatial_qkv, temporal_qkv, cotangent, spatial_gate, temporal_gate, temporal_proj, live_counts
):
    spatial = spatial_qkv[0]
    temporal = temporal_qkv[0]
    incoming = cotangent[0]
    frame_count, position_count, width = incoming.shape
    group_size = lax.axis_size("seq")
    member = lax.axis_index("seq")
    live_frames = live_counts[0, 0]
    live_positions = live_counts[0, 1]
    frame_ids = member * frame_count + jnp.arange(frame_count, dtype=jnp.int32)
    position_ids = jnp.arange(position_count, dtype=jnp.int32)
    token_mask = (
        (frame_ids[:, None] < live_frames) & (position_ids[None, :] < live_positions)
    ).astype(jnp.float32)
    flowing = token_mask[:, :, None] * incoming.astype(jnp.float32)
    temporal_error = (flowing * temporal_gate[0]).astype(jnp.bfloat16)
    temporal_back = lax.dot_general(
        temporal_error, temporal_proj, (((2,), (1,)), ((), ())), preferred_element_type=jnp.float32
    ).astype(jnp.bfloat16)
    stacked = jnp.concatenate([temporal, temporal_back[None]], axis=0)
    exchanged = lax.all_to_all(stacked, "seq", split_axis=2, concat_axis=1, tiled=True)
    spatial_keep = position_ids[None, :] < live_positions
    spatial_out = attend(
        spatial[0], spatial[1], spatial[2], spatial_keep, "bqhd,bkhd->bhqk", "bhqk,bkhd->bqhd"
    ).astype(jnp.bfloat16)
    total_frames = exchanged.shape[1]
    slice_positions = exchanged.shape[2]
    temporal_keep = jnp.broadcast_to(
        jnp.arange(total_frames, dtype=jnp.int32)[None, :] < live_frames,
        (slice_positions, total_frames),
    )

    def temporal_attend(queries, key_block, value_block):
        return attend(
            queries, key_block, value_block, temporal_keep, "qbhd,kbhd->bhqk", "bhqk,kbhd->qbhd"
        )

    temporal_result, pullback = jax.vjp(temporal_attend, exchanged[0], exchanged[1], exchanged[2])
    temporal_out = temporal_result.astype(jnp.bfloat16)
    input_grads = jnp.stack(pullback(exchanged[3].astype(jnp.float32)))
    temporal_frames = lax.all_to_all(temporal_out, "seq", split_axis=0, concat_axis=1, tiled=True)
    grads_home = lax.all_to_all(input_grads, "seq", split_axis=1, concat_axis=2, tiled=True)
    tokens = frame_count * position_count
    flat_spatial = spatial_out.reshape(tokens, width)
    flat_temporal = temporal_frames.reshape(tokens, width)
    slice_width = width // group_size
    column_spatial, column_temporal = (
        lax.all_to_all(flat_spatial, "seq", split_axis=1, concat_axis=0, tiled=True),
        lax.all_to_all(flat_temporal, "seq", split_axis=1, concat_axis=0, tiled=True),
    )
    spatial_scale = spatial_gate[0]
    temporal_scale = temporal_gate[0]
    starting = jnp.zeros((slice_width, 2, width), jnp.float32)
    cot_piece = lax.all_gather(incoming.reshape(tokens, width), "seq", axis=0, tiled=True)
    shards = cot_piece.shape[0] // tokens

    def one_block(block, total):
        offset = (block * tokens).astype(jnp.int32)
        rows = lax.dynamic_slice_in_dim(cot_piece, offset, tokens, 0)
        token_index = offset + jnp.arange(tokens, dtype=jnp.int32)
        frame_of = token_index // position_count
        position_of = token_index % position_count
        row_keep = ((frame_of < live_frames) & (position_of < live_positions)).astype(jnp.float32)
        masked_rows = row_keep[:, None] * rows.astype(jnp.float32)
        error_first = (masked_rows * spatial_scale).astype(jnp.bfloat16)
        error_second = (masked_rows * temporal_scale).astype(jnp.bfloat16)
        cols_first = lax.dynamic_slice_in_dim(column_spatial, offset, tokens, 0)
        cols_second = lax.dynamic_slice_in_dim(column_temporal, offset, tokens, 0)
        part_first = lax.dot_general(
            cols_first, error_first, (((0,), (0,)), ((), ())), preferred_element_type=jnp.float32
        )
        part_second = lax.dot_general(
            cols_second, error_second, (((0,), (0,)), ((), ())), preferred_element_type=jnp.float32
        )
        part_first = part_first.astype(jnp.bfloat16).astype(jnp.float32)
        part_second = part_second.astype(jnp.bfloat16).astype(jnp.float32)
        return total + jnp.stack([part_first, part_second], axis=1)

    partial_sum = lax.fori_loop(0, shards, one_block, starting)
    summed = lax.psum_scatter(partial_sum, "dp", scatter_dimension=2, tiled=True)
    return (grads_home[None], summed[:, 0], summed[:, 1])


def solution(mesh):
    return jax.shard_map(
        body,
        mesh=mesh,
        in_specs=(
            P("dp", None, "seq", None, None),
            P("dp", None, "seq", None, None),
            P("dp", "seq", None, None),
            P("dp", None),
            P("dp", None),
            P(),
            P("dp", None),
        ),
        out_specs=(P("dp", None, "seq", None, None), P("seq", "dp"), P("seq", "dp")),
        check_vma=False,
    )
```

profile of v0, /device:TPU:0, one launch (start us, length us, event | category | flops | bytes accessed | tf_op | source)
XLA Modules:
  0.0 223.8 jit_solution(1551317566120722395)
XLA Ops:
  7.9 1.6 fusion.49
  11.5 1.9 fusion.13
  14.6 2.2 pad_maximum_fusion
  16.9 4.3 %all-to-all-start = ((bf16[4,1,128,1152]{3,0,1,2:T(4,128)(2,1)}), bf16[4,1,128,1152]{3,0,1,2:T(4,128)(2,1)}, u32[]{:S(2)}, u32[]{:S(2)}) async-start(bf16[4,1,128,1152]{3,0,1,2:T(4,128)(2,1)} %pad_maximum_fusion), calls=%async_computation | async-start | bytes 2359296 | tf_op jit(solution)/shard_map/all_to_all | solution.py:48
  25.7 2.2 fusion.51
  27.9 1.3 fusion.17
  29.2 11.8 %all-to-all-done = bf16[4,1,128,1152]{3,0,1,2:T(4,128)(2,1)} async-done(((bf16[4,1,128,1152]{3,0,1,2:T(4,128)(2,1)}), bf16[4,1,128,1152]{3,0,1,2:T(4,128)(2,1)}, u32[]{:S(2)}, u32[]{:S(2)}) %all-to-all-start) | async-done | bytes 1179680 | tf_op jit(solution)/shard_map/all_to_all | solution.py:48
  41.0 9.7 %slice_reduce_fusion.2 = (bf16[128,1152]{1,0:T(8,128)(2,1)}, bf16[128,1152]{1,0:T(8,128)(2,1)S(1)}, bf16[128,1152]{1,0:T(8,128)(2,1)S(1)}, bf16[128,1152]{1,0:T(8,128)(2,1)S(1)}) fusion(bf16[4,1,128,1152]{3,0,1,2:T(4,128)(2,1)} %all-to-all-done), kind=kLoop, calls=%fused_computation.59 | loop fusion | bytes 2359296 | tf_op jit(solution)/shard_map/slice | solution.py:65
  50.7 2.7 %reshape_squeeze.6 = bf16[4,32,16,72]{3,2,1,0:T(8,128)(2,1)} reshape(bf16[128,1152]{1,0:T(8,128)(2,1)} %get-tuple-element.293) | data formatting | bytes 589824 | tf_op jit(solution)/shard_map/jvp()/reshape;squeeze | solution.py:14
  53.4 1.7 reshape_squeeze.15
  55.1 1.7 reshape_squeeze.14
  57.8 2.8 %fusion.50 = (f32[32,16,4]{2,1,0:T(8,128)S(1)}, f32[32,16,4,4]{2,3,1,0:T(4,128)S(1)}) fusion(bf16[4,32,16,72]{3,2,1,0:T(8,128)(2,1)} %reshape_squeeze.15, bf16[4,32,16,72]{3,2,1,0:T(8,128)(2,1)} %reshape_squeeze.14, pred[4]{0:T(512)(128)(4,1)S(1)} %iota_compare_fusion.1), kind=kOutput, calls=%fused_computation.92 | convolution fusion | flops 1202176 | bytes 630788 | tf_op jit(solution)/shard_map/jvp(qbhd,kbhd->bhqk)/dot_general | solution.py:15
  61.6 3.8 %convert_reduce_fusion = (f32[32,16,4]{2,1,0:T(8,128)}, pred[32,16,4,4]{2,3,1,0:T(4,128)(4,1)}, f32[32,16,4]{2,1,0:T(8,128)S(1)}, bf16[32,16,4,4]{2,3,1,0:T(4,128)(2,1)S(1)}) fusion(f32[32,16,4,4]{2,3,1,0:T(4,128)S(1)} %get-tuple-element.329, f32[32,16,4]{2,1,0:T(8,128)S(1)} %get-tuple-element.328, f32[32,16,4]{2,1,0:T(8,128)S(1)} %multiply_divide_fusion, ...), kind=kOutput, calls=%fused_computation.53 | convolution fusion | flops 1249280 | bytes 679936 | tf_op jit(solution)/shard_map/transpose(jvp(bhqk,kbhd->qbhd))/dot_general | solution.py:22
  65.5 2.7 %fusion.46 = (f32[32,16,4]{2,1,0:T(8,128)}, f32[32,16,4,4]{2,3,1,0:T(4,128)}, bf16[32,16,4,4]{2,3,1,0:T(4,128)(2,1)S(1)}) fusion(f32[32,16,4,4]{2,3,1,0:T(4,128)S(1)} %get-tuple-element.329, f32[32,16,4]{2,1,0:T(8,128)S(1)} %get-tuple-element.328, f32[32,16,4]{2,1,0:T(8,128)S(1)} %neg.9, f32[32,16,4]{2,1,0:T(8,128)S(1)} %fusion.45, ...), kind=kLoop, calls=%fused_computation.89 | loop fusion | flops 63488 | bytes 131072 | tf_op jit(solution)/shard_map/transpose(jvp())/reduce_sum | solution.py:19
  69.1 1.2 convert_element_type.190
  70.4 3.5 %all-to-all-start.3 = ((bf16[4,32,1152]{2,1,0:T(8,128)(2,1)}), bf16[4,32,1152]{2,1,0:T(8,128)(2,1)S(1)}, u32[]{:S(2)}, u32[]{:S(2)}) async-start(bf16[4,32,1152]{2,1,0:T(8,128)(2,1)} %convert_element_type.190), calls=%async_computation.3 | async-start | bytes 589824 | tf_op jit(solution)/shard_map/all_to_all | solution.py:68
  73.8 2.7 %convolution_convert_fusion.8 = bf16[16,128,72]{1,2,0:T(8,128)(2,1)} fusion(bf16[128,16,72]{0,2,1:T(8,128)(2,1)S(1)} %bitcast.87, f32[16,128]{1,0:T(8,128)S(1)} %copy-done.14, f32[16,128,128]{1,2,0:T(8,128)} %fusion.17), kind=kOutput, calls=%fused_computation.44 | convolution fusion | flops 38684800 | bytes 1646592 | tf_op jit(solution)/shard_map/bhqk,bkhd->bqhd/dot_general | solution.py:22
  76.5 3.6 %all-to-all-done.3 = bf16[4,32,1152]{2,1,0:T(8,128)(2,1)S(1)} async-done(((bf16[4,32,1152]{2,1,0:T(8,128)(2,1)}), bf16[4,32,1152]{2,1,0:T(8,128)(2,1)S(1)}, u32[]{:S(2)}, u32[]{:S(2)}) %all-to-all-start.3) | async-done | bytes 294944 | tf_op jit(solution)/shard_map/all_to_all | solution.py:68
  80.9 3.5 %all-to-all-start.2 = ((bf16[128,4,288]{0,2,1:T(8,128)(2,1)}), bf16[128,4,288]{0,2,1:T(8,128)(2,1)S(1)}, u32[]{:S(2)}, u32[]{:S(2)}) async-start(bf16[128,4,288]{0,2,1:T(8,128)(2,1)} %bitcast.88), calls=%async_computation.2 | async-start | bytes 589824 | tf_op jit(solution)/shard_map/all_to_all | solution.py:75
  84.3 1.3 all_to_all.53
  86.6 4.0 %all-to-all-done.2 = bf16[128,4,288]{0,2,1:T(8,128)(2,1)S(1)} async-done(((bf16[128,4,288]{0,2,1:T(8,128)(2,1)}), bf16[128,4,288]{0,2,1:T(8,128)(2,1)S(1)}, u32[]{:S(2)}, u32[]{:S(2)}) %all-to-all-start.2) | async-done | bytes 294944 | tf_op jit(solution)/shard_map/all_to_all | solution.py:75
  90.6 4.1 %all-to-all-start.4 = ((bf16[128,4,288]{0,2,1:T(8,128)(2,1)}), bf16[128,4,288]{0,2,1:T(8,128)(2,1)}, u32[]{:S(2)}, u32[]{:S(2)}) async-start(bf16[128,4,288]{0,2,1:T(8,128)(2,1)} %copy.110), calls=%async_computation.4 | async-start | bytes 589824 | tf_op jit(solution)/shard_map/all_to_all | solution.py:76
  95.3 5.9 %all-to-all-done.4 = bf16[128,4,288]{0,2,1:T(8,128)(2,1)} async-done(((bf16[128,4,288]{0,2,1:T(8,128)(2,1)}), bf16[128,4,288]{0,2,1:T(8,128)(2,1)}, u32[]{:S(2)}, u32[]{:S(2)}) %all-to-all-start.4) | async-done | bytes 294944 | tf_op jit(solution)/shard_map/all_to_all | solution.py:76
  102.4 29.1 %while.16 = (s32[]{:T(128)}, f32[288,2,1152]{2,0,1:T(8,128)}, bf16[512,288]{1,0:T(8,128)(2,1)S(1)}, s32[]{:T(128)}, s32[]{:T(128)}, /*index=5*/bf16[512,1152]{1,...) while((s32[]{:T(128)}, f32[288,2,1152]{2,0,1:T(8,128)}, ...), condition=%wide.region_8.9_spmd.clone, body=%wide.region_7.8_spmd.clone.sunk | while | flops 174369792 | bytes 8787673 | solution.py:106
  102.4 1.3 and_convert_fusion.3
  103.8 1.4 fusion.68
  105.1 1.4 fusion.67
  106.5 1.9 select_add_fusion.2
  108.4 1.3 and_convert_fusion.3
  109.7 1.4 fusion.68
  111.1 1.4 fusion.67
  112.5 3.6 %select_add_fusion.2 = f32[288,2,1152]{2,0,1:T(8,128)} fusion(f32[288,2,1152]{2,0,1:T(8,128)} %get-tuple-element.403, bf16[288,1,1152]{2,0,1:T(8,128)(2,1)S(1)} %fusion.67, bf16[288,1,1152]{2,0,1:T(8,128)(2,1)S(1)} %fusion.68, pred[]{:T(512)S(6)} %compare.19), kind=kLoop, calls=%fused_computation.clone.1 | loop fusion | flops 2654208 | bytes 6635521 | tf_op jit(solution)/shard_map/while/body/eval_jaxpr/add | solution.py:104
  116.1 1.3 and_convert_fusion.3
  117.4 1.4 fusion.68
  118.8 1.4 fusion.67
  120.2 3.6 %select_add_fusion.2 = f32[288,2,1152]{2,0,1:T(8,128)} fusion(f32[288,2,1152]{2,0,1:T(8,128)} %get-tuple-element.403, bf16[288,1,1152]{2,0,1:T(8,128)(2,1)S(1)} %fusion.67, bf16[288,1,1152]{2,0,1:T(8,128)(2,1)S(1)} %fusion.68, pred[]{:T(512)S(6)} %compare.19), kind=kLoop, calls=%fused_computation.clone.1 | loop fusion | flops 2654208 | bytes 6635521 | tf_op jit(solution)/shard_map/while/body/eval_jaxpr/add | solution.py:104
  123.8 1.3 and_convert_fusion.3
  125.1 1.4 fusion.68
  126.5 1.4 fusion.67
  127.9 3.6 %select_add_fusion.2 = f32[288,2,1152]{2,0,1:T(8,128)} fusion(f32[288,2,1152]{2,0,1:T(8,128)} %get-tuple-element.403, bf16[288,1,1152]{2,0,1:T(8,128)(2,1)S(1)} %fusion.67, bf16[288,1,1152]{2,0,1:T(8,128)(2,1)S(1)} %fusion.68, pred[]{:T(512)S(6)} %compare.19), kind=kLoop, calls=%fused_computation.clone.1 | loop fusion | flops 2654208 | bytes 6635521 | tf_op jit(solution)/shard_map/while/body/eval_jaxpr/add | solution.py:104
  131.5 3.6 %copy.113 = f32[288,2,1152]{0,2,1:T(8,128)} copy(f32[288,2,1152]{2,0,1:T(8,128)} %get-tuple-element.226) | data formatting | bytes 5308416 | tf_op jit(solution)/shard_map/while | solution.py:106
  137.1 2.6 %fusion.18 = bf16[4,32,16,72]{3,0,2,1:T(4,128)(2,1)S(1)} fusion(bf16[4,32,16,72]{3,2,1,0:T(8,128)(2,1)S(1)} %copy-done.7, f32[32,16,4,4]{2,3,1,0:T(4,128)} %get-tuple-element.316, pred[32,16,4,4]{2,3,1,0:T(4,128)(4,1)} %get-tuple-element.318, f32[32,16,4]{2,1,0:T(8,128)S(1)} %negate_divide_fusion, pred[4]{0:T(512)(128)(4,1)S(1)} %iota_compare_fusion.1), kind=kOutput, calls=%fused_computation.40 | convolution fusion | flops 1359872 | bytes 638980 | tf_op jit(solution)/shard_map/transpose(jvp(qbhd,kbhd->bhqk))/dot_general | solution.py:15
  140.3 2.6 %fusion.19 = bf16[4,32,16,72]{3,0,2,1:T(4,128)(2,1)S(1)} fusion(bf16[4,32,16,72]{3,2,1,0:T(8,128)(2,1)} %reshape_squeeze.14, f32[32,16,4,4]{2,3,1,0:T(4,128)} %get-tuple-element.316, pred[32,16,4,4]{2,3,1,0:T(4,128)(4,1)} %get-tuple-element.318, f32[32,16,4]{2,1,0:T(8,128)} %copy-done.11, pred[4]{0:T(512)(128)(4,1)S(1)} %iota_compare_fusion.1), kind=kOutput, calls=%fused_computation.41 | convolution fusion | flops 1359872 | bytes 638980 | tf_op jit(solution)/shard_map/transpose(jvp(qbhd,kbhd->bhqk))/dot_general | solution.py:15
  144.3 1.9 fusion.20
  146.2 1.2 reshape.203
  148.7 15.1 %all_to_all.62 = bf16[3,4,32,1152]{3,2,0,1:T(8,128)(2,1)S(1)} all-to-all(bf16[3,4,32,1152]{3,2,0,1:T(8,128)(2,1)S(1)} %copy.100), channel_id=1, replica_groups=mesh['dp'=8,'seq'=4] {'seq'}, dimensions={1} | all-to-all | bytes 1769472 | tf_op jit(solution)/shard_map/all_to_all | solution.py:69
  164.8 50.3 %reduce-scatter.2.cloned.1.call-done = f32[288,2,144]{0,2,1:T(8,128)} async-done(((f32[288,2,1152]{0,2,1:T(8,128)}), f32[288,2,144]{0,2,1:T(8,128)}) %reduce-scatter.2.cloned.1.call-update) | async-done | bytes 331792 | tf_op jit(solution)/shard_map/reduce_scatter | solution.py:107
  215.1 1.8 slice_bitcast_fusion
  (71 shorter events, 20.4 us)
Async XLA Ops:
  7.2 4.3 %copy-start = (bf16[1152,1152]{1,0:T(8,128)(2,1)S(1)}, bf16[1152,1152]{1,0:T(8,128)(2,1)}, u32[]{:S(2)}) copy-start(bf16[1152,1152]{1,0:T(8,128)(2,1)} %param.14) | copy-start | bytes 7962628
  7.2 6.7 %copy-start.5 = (bf16[1,3,1,128,1152]{4,3,2,1,0:T(8,128)(2,1)S(1)}, bf16[1,3,1,128,1152]{4,3,2,1,0:T(8,128)(2,1)}, u32[]{:S(2)}) copy-start(bf16[1,3,1,128,1152]{4,3,2,1,0:T(8,128)(2,1)} %param.10) | copy-start | bytes 2654212
  7.2 95.2 %all-gather.3.cloned.1.call-start = ((), (), s32[]{:S(2)}) async-start(), calls=%async_computation.7 | async-start | bytes 1474560 | tf_op jit(solution)/shard_map/all_gather | solution.py:81
  16.9 24.1 %all-to-all-start = ((bf16[4,1,128,1152]{3,0,1,2:T(4,128)(2,1)}), bf16[4,1,128,1152]{3,0,1,2:T(4,128)(2,1)}, u32[]{:S(2)}, u32[]{:S(2)}) async-start(bf16[4,1,128,1152]{3,0,1,2:T(4,128)(2,1)} %pad_maximum_fusion), calls=%async_computation | async-start | bytes 2359296 | tf_op jit(solution)/shard_map/all_to_all | solution.py:48
  23.3 4.6 %copy-start.2 = (bf16[1,1,1,128,1152]{3,4,2,1,0:T(8,128)(2,1)S(1)}, bf16[1,1,1,128,1152]{3,4,2,1,0:T(8,128)(2,1)}, u32[]{:S(2)}) copy-start(bf16[1,1,1,128,1152]{3,4,2,1,0:T(8,128)(2,1)} %copy.103) | copy-start | bytes 884740
  24.2 3.7 %copy-start.3 = (bf16[1,1,1,128,1152]{3,4,2,1,0:T(8,128)(2,1)S(1)}, bf16[1,1,1,128,1152]{3,4,2,1,0:T(8,128)(2,1)}, u32[]{:S(2)}) copy-start(bf16[1,1,1,128,1152]{3,4,2,1,0:T(8,128)(2,1)} %copy.102) | copy-start | bytes 884740
  57.8 3.8 %copy-start.6 = (bf16[4,32,16,72]{3,2,1,0:T(8,128)(2,1)}, bf16[4,32,16,72]{3,2,1,0:T(8,128)(2,1)S(1)}, u32[]{:S(2)}) copy-start(bf16[4,32,16,72]{3,2,1,0:T(8,128)(2,1)S(1)} %reshape.200) | copy-start | bytes 884740
  57.8 3.8 %copy-start.8 = (bf16[4,32,16,72]{3,2,1,0:T(8,128)(2,1)S(1)}, bf16[4,32,16,72]{3,2,1,0:T(8,128)(2,1)}, u32[]{:S(2)}) copy-start(bf16[4,32,16,72]{3,2,1,0:T(8,128)(2,1)} %reshape_squeeze.6) | copy-start | bytes 884740
  68.2 0.9 copy-start.9
  68.2 5.6 %copy-start.10 = (bf16[1,1,1,128,1152]{3,4,2,1,0:T(8,128)(2,1)S(1)}, bf16[1,1,1,128,1152]{3,4,2,1,0:T(8,128)(2,1)}, u32[]{:S(2)}) copy-start(bf16[1,1,1,128,1152]{3,4,2,1,0:T(8,128)(2,1)} %copy.104) | copy-start | bytes 884740
  68.2 5.6 %copy-start.14 = (f32[16,128]{1,0:T(8,128)S(1)}, f32[16,128]{1,0:T(8,128)}, u32[]{:S(2)}) copy-start(f32[16,128]{1,0:T(8,128)} %fusion.51) | copy-start | bytes 24580
  70.4 9.8 %all-to-all-start.3 = ((bf16[4,32,1152]{2,1,0:T(8,128)(2,1)}), bf16[4,32,1152]{2,1,0:T(8,128)(2,1)S(1)}, u32[]{:S(2)}, u32[]{:S(2)}) async-start(bf16[4,32,1152]{2,1,0:T(8,128)(2,1)} %convert_element_type.190), calls=%async_computation.3 | async-start | bytes 589824 | tf_op jit(solution)/shard_map/all_to_all | solution.py:68
  76.5 25.8 %copy-start.12 = (f32[1,1152]{1,0:T(1,128)S(1)}, f32[1,1152]{1,0:T(1,128)}, u32[]{:S(2)}) copy-start(f32[1,1152]{1,0:T(1,128)} %param.13) | copy-start | bytes 13828
  76.5 25.8 %copy-start.13 = (f32[1,1152]{1,0:T(1,128)S(1)}, f32[1,1152]{1,0:T(1,128)}, u32[]{:S(2)}) copy-start(f32[1,1152]{1,0:T(1,128)} %param.12) | copy-start | bytes 13828
  80.1 0.7 copy-start.1
  80.9 9.8 %all-to-all-start.2 = ((bf16[128,4,288]{0,2,1:T(8,128)(2,1)}), bf16[128,4,288]{0,2,1:T(8,128)(2,1)S(1)}, u32[]{:S(2)}, u32[]{:S(2)}) async-start(bf16[128,4,288]{0,2,1:T(8,128)(2,1)} %bitcast.88), calls=%async_computation.2 | async-start | bytes 589824 | tf_op jit(solution)/shard_map/all_to_all | solution.py:75
  90.6 10.5 %all-to-all-start.4 = ((bf16[128,4,288]{0,2,1:T(8,128)(2,1)}), bf16[128,4,288]{0,2,1:T(8,128)(2,1)}, u32[]{:S(2)}, u32[]{:S(2)}) async-start(bf16[128,4,288]{0,2,1:T(8,128)(2,1)} %copy.110), calls=%async_computation.4 | async-start | bytes 589824 | tf_op jit(solution)/shard_map/all_to_all | solution.py:76
  94.8 120.4 %reduce-scatter.2.cloned.1.call-start = ((), (), s32[]{:S(2)}) async-start(), calls=%async_computation.6 | async-start | bytes 3981312 | tf_op jit(solution)/shard_map/reduce_scatter | solution.py:107
  135.1 0.9 copy-start.4
  135.1 2.0 copy-start.7
  137.1 2.7 %copy-start.11 = (f32[32,16,4]{2,1,0:T(8,128)}, f32[32,16,4]{2,1,0:T(8,128)S(1)}, u32[]{:S(2)}) copy-start(f32[32,16,4]{2,1,0:T(8,128)S(1)} %negate_divide_fusion) | copy-start | bytes 24580
Sparse Core Ops, SparseCore 0:
  9.6 23.3 all-gather.2
  135.3 79.7 reduce-scatter.1
where the time goes:
time: 225 us; the launch traced here: 224 us
  waiting for transfers between devices  76.3 us (34%)
  local copies, waits for them, and re-layouts  39.9 us (18%)
  matrix products  33.7 us (15%)
  other arithmetic  28 us (12%)
  starting transfers between devices  15.6 us (7%)
  blocking collectives  15.1 us (7%)
  between operations  15 us (7%)
    reduce_scatter x1, waiting for transfers between devices, body(): lax.psum_scatter(partial_sum, 'dp', scatter_dimension=2, tiled=True)  50.3 us
    all_to_all x1, blocking collectives, body(): lax.all_to_all(input_grads, 'seq', split_axis=1, concat_axis=2, tiled=True)  15.1 us
    add x4, other arithmetic, one_block(): return total + jnp.stack([part_first, part_second], axis=1)  12.6 us
    all_to_all x1, waiting for transfers between devices, body(): lax.all_to_all(stacked, 'seq', split_axis=2, concat_axis=1, tiled=True)  11.8 us
    slice x1, local copies, waits for them, and re-layouts, body(): exchanged[2]  9.68 us
    dot_general x4, matrix products, attend(): jnp.einsum(score_form, q_heads, k_heads, preferred_element_type=jnp.float32)  9.34 us
    dot_general x4, matrix products, attend(): jnp.einsum(mix_form, attention_weights, v_heads, preferred_element_type=j...  9.24 us
    all_to_all x1, waiting for transfers between devices, body(): lax.all_to_all(flat_temporal, 'seq', split_axis=1, concat_axis=0, tiled=T...  5.91 us
  transfers between devices with their start and end apart: 6, of which 5 were waited for; matrix products, arithmetic and copies ran while one was open for 29% of the time, Pallas kernels for 0%

commit v1 on v0

--- a/solution.py
+++ b/solution.py
@@ -45,7 +45,10 @@
         temporal_error, temporal_proj, (((2,), (1,)), ((), ())), preferred_element_type=jnp.float32
     ).astype(jnp.bfloat16)
     stacked = jnp.concatenate([temporal, temporal_back[None]], axis=0)
-    exchanged = lax.all_to_all(stacked, "seq", split_axis=2, concat_axis=1, tiled=True)
+    exchanged = jnp.concatenate(
+        lax.all_to_all(jnp.stack(jnp.split(stacked, lax.axis_size("seq"), axis=2)), "seq", 0, 0),
+        axis=1,
+    )
     spatial_keep = position_ids[None, :] < live_positions
     spatial_out = attend(
         spatial[0], spatial[1], spatial[2], spatial_keep, "bqhd,bkhd->bhqk", "bhqk,bkhd->bqhd"

time: 225 us -> 217 us (0.964)
  local copies, waits for them, and re-layouts: 39.9 us -> 31 us
  waiting for transfers between devices: 76.3 us -> 78.8 us
    slice x1, local copies, waits for them, and re-layouts: 9.68 us -> 2.05 us  [body(): exchanged[2]]
    all_to_all x1, waiting for transfers between devices: 11.8 us -> 14.7 us  [body(): lax.all_to_all(jnp.stack(jnp.split(stacked, lax.axis_size('seq'), axis=2)...]
  transfers between devices with their start and end apart: 6 -> 6, of which waited for: 5 -> 5; matrix products, arithmetic and copies ran while one was open for 29% -> 25% of each run, Pallas kernels for 0% -> 0%
where the time goes in v1:
time: 217 us; the launch traced here: 216 us
  waiting for transfers between devices  78.8 us (36%)
  matrix products  33 us (15%)
  local copies, waits for them, and re-layouts  31 us (14%)
  other arithmetic  27.2 us (13%)
  starting transfers between devices  15.5 us (7%)
  blocking collectives  15.1 us (7%)
  between operations  15 us (7%)
    reduce_scatter x1, waiting for transfers between devices, body(): lax.psum_scatter(partial_sum, 'dp', scatter_dimension=2, tiled=True)  49.9 us
    all_to_all x1, blocking collectives, body(): lax.all_to_all(input_grads, 'seq', split_axis=1, concat_axis=2, tiled=True)  15.1 us
    all_to_all x1, waiting for transfers between devices, body(): lax.all_to_all(jnp.stack(jnp.split(stacked, lax.axis_size('seq'), axis=2)...  14.7 us
    add x4, other arithmetic, one_block(): return total + jnp.stack([part_first, part_second], axis=1)  12.7 us
    dot_general x4, matrix products, attend(): jnp.einsum(score_form, q_heads, k_heads, preferred_element_type=jnp.float32)  9.31 us
    dot_general x4, matrix products, attend(): jnp.einsum(mix_form, attention_weights, v_heads, preferred_element_type=j...  9.24 us
    all_to_all x1, waiting for transfers between devices, body(): lax.all_to_all(flat_temporal, 'seq', split_axis=1, concat_axis=0, tiled=T...  6.13 us
    dot_general x4, matrix products, one_block(): lax.dot_general(cols_first, error_first, (((0,), (0,)), ((), ())), prefer...  5.51 us
  transfers between devices with their start and end apart: 6, of which 5 were waited for; matrix products, arithmetic and copies ran while one was open for 25% of the time, Pallas kernels for 0%

profile of v1, /device:TPU:0, one launch (start us, length us, event | category | flops | bytes accessed | tf_op | source)
XLA Modules:
  0.0 215.8 jit_solution(14869628687250926888)
XLA Ops:
  7.9 1.3 fusion.57
  11.3 2.0 fusion.13
  14.6 4.3 %all-to-all-start = ((bf16[4,4,1,32,1152]{4,3,1,2,0:T(8,128)(2,1)}), bf16[4,4,1,32,1152]{4,3,1,2,0:T(8,128)(2,1)}, u32[]{:S(2)}, u32[]{:S(2)}) async-start(bf16[4,4,1,32,1152]{4,3,1,2,0:T(8,128)(2,1)} %pad_maximum_fusion), calls=%async_computation | async-start | bytes 2359296 | tf_op jit(solution)/shard_map/all_to_all | solution.py:49
  23.5 1.5 fusion.59
  25.0 1.3 fusion.17
  26.3 14.7 %all-to-all-done = bf16[4,4,1,32,1152]{4,3,1,2,0:T(8,128)(2,1)} async-done(((bf16[4,4,1,32,1152]{4,3,1,2,0:T(8,128)(2,1)}), bf16[4,4,1,32,1152]{4,3,1,2,0:T(8,128)(2,1)}, u32[]{:S(2)}, u32[]{:S(2)}) %all-to-all-start) | async-done | bytes 1179680 | tf_op jit(solution)/shard_map/all_to_all | solution.py:49
  41.0 2.0 fusion.55
  43.0 2.7 %reshape_squeeze.6 = bf16[4,32,16,72]{3,2,1,0:T(8,128)(2,1)} reshape(bf16[1,4,1,32,1152]{4,3,0,2,1:T(8,128)(2,1)} %get-tuple-element.317) | data formatting | bytes 589824 | tf_op jit(solution)/shard_map/jvp()/reshape;squeeze | solution.py:14
  45.8 1.7 reshape_squeeze.15
  47.5 1.8 reshape_squeeze.14
  50.2 2.7 %fusion.58 = (f32[32,16,4]{2,1,0:T(8,128)S(1)}, f32[32,16,4,4]{2,3,1,0:T(4,128)S(1)}) fusion(bf16[4,32,16,72]{3,2,1,0:T(8,128)(2,1)} %reshape_squeeze.15, bf16[4,32,16,72]{3,2,1,0:T(8,128)(2,1)} %reshape_squeeze.14, pred[4]{0:T(512)(128)(4,1)S(1)} %iota_compare_fusion.1), kind=kOutput, calls=%fused_computation.102 | convolution fusion | flops 1202176 | bytes 630788 | tf_op jit(solution)/shard_map/jvp(qbhd,kbhd->bhqk)/dot_general | solution.py:15
  54.0 3.9 %convert_reduce_fusion = (f32[32,16,4]{2,1,0:T(8,128)}, pred[32,16,4,4]{2,3,1,0:T(4,128)(4,1)}, f32[32,16,4]{2,1,0:T(8,128)S(1)}, bf16[32,16,4,4]{2,3,1,0:T(4,128)(2,1)S(1)}) fusion(f32[32,16,4,4]{2,3,1,0:T(4,128)S(1)} %get-tuple-element.333, f32[32,16,4]{2,1,0:T(8,128)S(1)} %get-tuple-element.332, f32[32,16,4]{2,1,0:T(8,128)S(1)} %multiply_divide_fusion, ...), kind=kOutput, calls=%fused_computation.58 | convolution fusion | flops 1249280 | bytes 679936 | tf_op jit(solution)/shard_map/transpose(jvp(bhqk,kbhd->qbhd))/dot_general | solution.py:22
  57.9 2.7 %fusion.53 = (f32[32,16,4]{2,1,0:T(8,128)}, f32[32,16,4,4]{2,3,1,0:T(4,128)}, bf16[32,16,4,4]{2,3,1,0:T(4,128)(2,1)S(1)}) fusion(f32[32,16,4,4]{2,3,1,0:T(4,128)S(1)} %get-tuple-element.333, f32[32,16,4]{2,1,0:T(8,128)S(1)} %get-tuple-element.332, f32[32,16,4]{2,1,0:T(8,128)S(1)} %neg.9, f32[32,16,4]{2,1,0:T(8,128)S(1)} %fusion.52, ...), kind=kLoop, calls=%fused_computation.98 | loop fusion | flops 63488 | bytes 131072 | tf_op jit(solution)/shard_map/transpose(jvp())/reduce_sum | solution.py:19
  61.5 1.3 convert_element_type.190
  62.8 3.6 %all-to-all-start.3 = ((bf16[4,32,1152]{2,1,0:T(8,128)(2,1)}), bf16[4,32,1152]{2,1,0:T(8,128)(2,1)S(1)}, u32[]{:S(2)}, u32[]{:S(2)}) async-start(bf16[4,32,1152]{2,1,0:T(8,128)(2,1)} %convert_element_type.190), calls=%async_computation.3 | async-start | bytes 589824 | tf_op jit(solution)/shard_map/all_to_all | solution.py:71
  66.5 2.7 %convolution_convert_fusion.8 = bf16[16,128,72]{1,2,0:T(8,128)(2,1)} fusion(bf16[128,16,72]{0,2,1:T(8,128)(2,1)S(1)} %bitcast.112, f32[16,128]{1,0:T(8,128)S(1)} %fusion.59, f32[16,128,128]{1,2,0:T(8,128)} %fusion.17), kind=kOutput, calls=%fused_computation.47 | convolution fusion | flops 38684800 | bytes 1646592 | tf_op jit(solution)/shard_map/bhqk,bkhd->bqhd/dot_general | solution.py:22
  69.1 3.4 %all-to-all-done.3 = bf16[4,32,1152]{2,1,0:T(8,128)(2,1)S(1)} async-done(((bf16[4,32,1152]{2,1,0:T(8,128)(2,1)}), bf16[4,32,1152]{2,1,0:T(8,128)(2,1)S(1)}, u32[]{:S(2)}, u32[]{:S(2)}) %all-to-all-start.3) | async-done | bytes 294944 | tf_op jit(solution)/shard_map/all_to_all | solution.py:71
  73.3 3.5 %all-to-all-start.2 = ((bf16[128,4,288]{0,2,1:T(8,128)(2,1)}), bf16[128,4,288]{0,2,1:T(8,128)(2,1)S(1)}, u32[]{:S(2)}, u32[]{:S(2)}) async-start(bf16[128,4,288]{0,2,1:T(8,128)(2,1)} %bitcast.113), calls=%async_computation.2 | async-start | bytes 589824 | tf_op jit(solution)/shard_map/all_to_all | solution.py:78
  76.8 1.3 all_to_all.49
  79.1 4.0 %all-to-all-done.2 = bf16[128,4,288]{0,2,1:T(8,128)(2,1)S(1)} async-done(((bf16[128,4,288]{0,2,1:T(8,128)(2,1)}), bf16[128,4,288]{0,2,1:T(8,128)(2,1)S(1)}, u32[]{:S(2)}, u32[]{:S(2)}) %all-to-all-start.2) | async-done | bytes 294944 | tf_op jit(solution)/shard_map/all_to_all | solution.py:78
  83.1 4.1 %all-to-all-start.4 = ((bf16[128,4,288]{0,2,1:T(8,128)(2,1)}), bf16[128,4,288]{0,2,1:T(8,128)(2,1)}, u32[]{:S(2)}, u32[]{:S(2)}) async-start(bf16[128,4,288]{0,2,1:T(8,128)(2,1)} %copy.108), calls=%async_computation.4 | async-start | bytes 589824 | tf_op jit(solution)/shard_map/all_to_all | solution.py:79
  87.5 6.1 %all-to-all-done.4 = bf16[128,4,288]{0,2,1:T(8,128)(2,1)} async-done(((bf16[128,4,288]{0,2,1:T(8,128)(2,1)}), bf16[128,4,288]{0,2,1:T(8,128)(2,1)}, u32[]{:S(2)}, u32[]{:S(2)}) %all-to-all-start.4) | async-done | bytes 294944 | tf_op jit(solution)/shard_map/all_to_all | solution.py:79
  94.8 29.1 %while.16 = (s32[]{:T(128)}, f32[288,2,1152]{2,0,1:T(8,128)}, bf16[512,288]{1,0:T(8,128)(2,1)S(1)}, s32[]{:T(128)}, s32[]{:T(128)}, /*index=5*/bf16[512,1152]{1,...) while((s32[]{:T(128)}, f32[288,2,1152]{2,0,1:T(8,128)}, ...), condition=%wide.region_8.9_spmd.clone, body=%wide.region_7.8_spmd.clone.sunk | while | flops 174369792 | bytes 8787673 | solution.py:109
  94.9 1.3 and_convert_fusion.3
  96.2 1.4 fusion.76
  97.6 1.4 fusion.75
  99.0 1.9 select_add_fusion.2
  100.8 1.3 and_convert_fusion.3
  102.2 1.4 fusion.76
  103.6 1.4 fusion.75
  104.9 3.6 %select_add_fusion.2 = f32[288,2,1152]{2,0,1:T(8,128)} fusion(f32[288,2,1152]{2,0,1:T(8,128)} %get-tuple-element.407, bf16[288,1,1152]{2,0,1:T(8,128)(2,1)S(1)} %fusion.75, bf16[288,1,1152]{2,0,1:T(8,128)(2,1)S(1)} %fusion.76, pred[]{:T(512)S(6)} %compare.19), kind=kLoop, calls=%fused_computation.clone.1 | loop fusion | flops 2654208 | bytes 6635521 | tf_op jit(solution)/shard_map/while/body/eval_jaxpr/add | solution.py:107
  108.6 1.3 and_convert_fusion.3
  109.9 1.4 fusion.76
  111.3 1.4 fusion.75
  112.7 3.6 %select_add_fusion.2 = f32[288,2,1152]{2,0,1:T(8,128)} fusion(f32[288,2,1152]{2,0,1:T(8,128)} %get-tuple-element.407, bf16[288,1,1152]{2,0,1:T(8,128)(2,1)S(1)} %fusion.75, bf16[288,1,1152]{2,0,1:T(8,128)(2,1)S(1)} %fusion.76, pred[]{:T(512)S(6)} %compare.19), kind=kLoop, calls=%fused_computation.clone.1 | loop fusion | flops 2654208 | bytes 6635521 | tf_op jit(solution)/shard_map/while/body/eval_jaxpr/add | solution.py:107
  116.3 1.3 and_convert_fusion.3
  117.6 1.4 fusion.76
  119.0 1.4 fusion.75
  120.4 3.6 %select_add_fusion.2 = f32[288,2,1152]{2,0,1:T(8,128)} fusion(f32[288,2,1152]{2,0,1:T(8,128)} %get-tuple-element.407, bf16[288,1,1152]{2,0,1:T(8,128)(2,1)S(1)} %fusion.75, bf16[288,1,1152]{2,0,1:T(8,128)(2,1)S(1)} %fusion.76, pred[]{:T(512)S(6)} %compare.19), kind=kLoop, calls=%fused_computation.clone.1 | loop fusion | flops 2654208 | bytes 6635521 | tf_op jit(solution)/shard_map/while/body/eval_jaxpr/add | solution.py:107
  124.0 3.6 %copy.111 = f32[288,2,1152]{0,2,1:T(8,128)} copy(f32[288,2,1152]{2,0,1:T(8,128)} %get-tuple-element.226) | data formatting | bytes 5308416 | tf_op jit(solution)/shard_map/while | solution.py:109
  129.6 2.6 %fusion.18 = bf16[4,32,16,72]{3,0,2,1:T(4,128)(2,1)S(1)} fusion(bf16[4,32,16,72]{3,2,1,0:T(8,128)(2,1)S(1)} %copy-done.7, f32[32,16,4,4]{2,3,1,0:T(4,128)} %get-tuple-element.312, pred[32,16,4,4]{2,3,1,0:T(4,128)(4,1)} %get-tuple-element.314, f32[32,16,4]{2,1,0:T(8,128)S(1)} %negate_divide_fusion, pred[4]{0:T(512)(128)(4,1)S(1)} %iota_compare_fusion.1), kind=kOutput, calls=%fused_computation.43 | convolution fusion | flops 1359872 | bytes 638980 | tf_op jit(solution)/shard_map/transpose(jvp(qbhd,kbhd->bhqk))/dot_general | solution.py:15
  132.8 2.6 %fusion.19 = bf16[4,32,16,72]{3,0,2,1:T(4,128)(2,1)S(1)} fusion(bf16[4,32,16,72]{3,2,1,0:T(8,128)(2,1)} %reshape_squeeze.14, f32[32,16,4,4]{2,3,1,0:T(4,128)} %get-tuple-element.312, pred[32,16,4,4]{2,3,1,0:T(4,128)(4,1)} %get-tuple-element.314, f32[32,16,4]{2,1,0:T(8,128)} %copy-done.11, pred[4]{0:T(512)(128)(4,1)S(1)} %iota_compare_fusion.1), kind=kOutput, calls=%fused_computation.44 | convolution fusion | flops 1359872 | bytes 638980 | tf_op jit(solution)/shard_map/transpose(jvp(qbhd,kbhd->bhqk))/dot_general | solution.py:15
  135.5 1.2 reshape.202
  136.8 1.9 fusion.20
  138.7 1.2 reshape.203
  141.2 15.1 %all_to_all.58 = bf16[3,4,32,1152]{3,2,0,1:T(8,128)(2,1)S(1)} all-to-all(bf16[3,4,32,1152]{3,2,0,1:T(8,128)(2,1)S(1)} %copy.98), channel_id=1, replica_groups=mesh['dp'=8,'seq'=4] {'seq'}, dimensions={1} | all-to-all | bytes 1769472 | tf_op jit(solution)/shard_map/all_to_all | solution.py:72
  157.3 49.9 %reduce-scatter.2.cloned.1.call-done = f32[288,2,144]{0,2,1:T(8,128)} async-done(((f32[288,2,1152]{0,2,1:T(8,128)}), f32[288,2,144]{0,2,1:T(8,128)}) %reduce-scatter.2.cloned.1.call-update) | async-done | bytes 331792 | tf_op jit(solution)/shard_map/reduce_scatter | solution.py:110
  207.2 1.8 slice_bitcast_fusion
  (68 shorter events, 19.2 us)
Async XLA Ops:
  7.2 4.1 %copy-start = (bf16[1152,1152]{1,0:T(8,128)(2,1)S(1)}, bf16[1152,1152]{1,0:T(8,128)(2,1)}, u32[]{:S(2)}) copy-start(bf16[1152,1152]{1,0:T(8,128)(2,1)} %param.14) | copy-start | bytes 7962628
  7.2 87.6 %all-gather.3.cloned.1.call-start = ((), (), s32[]{:S(2)}) async-start(), calls=%async_computation.7 | async-start | bytes 1474560 | tf_op jit(solution)/shard_map/all_gather | solution.py:84
  11.2 2.0 copy-start.5
  14.6 26.4 %all-to-all-start = ((bf16[4,4,1,32,1152]{4,3,1,2,0:T(8,128)(2,1)}), bf16[4,4,1,32,1152]{4,3,1,2,0:T(8,128)(2,1)}, u32[]{:S(2)}, u32[]{:S(2)}) async-start(bf16[4,4,1,32,1152]{4,3,1,2,0:T(8,128)(2,1)} %pad_maximum_fusion), calls=%async_computation | async-start | bytes 2359296 | tf_op jit(solution)/shard_map/all_to_all | solution.py:49
  21.0 2.5 %copy-start.2 = (bf16[1,1,1,128,1152]{3,4,2,1,0:T(8,128)(2,1)S(1)}, bf16[1,1,1,128,1152]{3,4,2,1,0:T(8,128)(2,1)}, u32[]{:S(2)}) copy-start(bf16[1,1,1,128,1152]{3,4,2,1,0:T(8,128)(2,1)} %copy.101) | copy-start | bytes 884740
  22.8 2.2 %copy-start.3 = (bf16[1,1,1,128,1152]{3,4,2,1,0:T(8,128)(2,1)S(1)}, bf16[1,1,1,128,1152]{3,4,2,1,0:T(8,128)(2,1)}, u32[]{:S(2)}) copy-start(bf16[1,1,1,128,1152]{3,4,2,1,0:T(8,128)(2,1)} %copy.100) | copy-start | bytes 884740
  50.2 3.8 %copy-start.6 = (bf16[4,32,16,72]{3,2,1,0:T(8,128)(2,1)}, bf16[4,32,16,72]{3,2,1,0:T(8,128)(2,1)S(1)}, u32[]{:S(2)}) copy-start(bf16[4,32,16,72]{3,2,1,0:T(8,128)(2,1)S(1)} %reshape.200) | copy-start | bytes 884740
  53.0 1.0 copy-start.8
  60.6 0.9 copy-start.9
  61.5 5.0 %copy-start.10 = (bf16[1,1,1,128,1152]{3,4,2,1,0:T(8,128)(2,1)S(1)}, bf16[1,1,1,128,1152]{3,4,2,1,0:T(8,128)(2,1)}, u32[]{:S(2)}) copy-start(bf16[1,1,1,128,1152]{3,4,2,1,0:T(8,128)(2,1)} %copy.102) | copy-start | bytes 884740
  62.8 9.8 %all-to-all-start.3 = ((bf16[4,32,1152]{2,1,0:T(8,128)(2,1)}), bf16[4,32,1152]{2,1,0:T(8,128)(2,1)S(1)}, u32[]{:S(2)}, u32[]{:S(2)}) async-start(bf16[4,32,1152]{2,1,0:T(8,128)(2,1)} %convert_element_type.190), calls=%async_computation.3 | async-start | bytes 589824 | tf_op jit(solution)/shard_map/all_to_all | solution.py:71
  72.6 0.7 copy-start.1
  73.3 9.8 %all-to-all-start.2 = ((bf16[128,4,288]{0,2,1:T(8,128)(2,1)}), bf16[128,4,288]{0,2,1:T(8,128)(2,1)S(1)}, u32[]{:S(2)}, u32[]{:S(2)}) async-start(bf16[128,4,288]{0,2,1:T(8,128)(2,1)} %bitcast.113), calls=%async_computation.2 | async-start | bytes 589824 | tf_op jit(solution)/shard_map/all_to_all | solution.py:78
  78.1 16.7 %copy-start.12 = (f32[1,1152]{1,0:T(1,128)S(1)}, f32[1,1152]{1,0:T(1,128)}, u32[]{:S(2)}) copy-start(f32[1,1152]{1,0:T(1,128)} %param.13) | copy-start | bytes 13828
  78.1 16.7 %copy-start.13 = (f32[1,1152]{1,0:T(1,128)S(1)}, f32[1,1152]{1,0:T(1,128)}, u32[]{:S(2)}) copy-start(f32[1,1152]{1,0:T(1,128)} %param.12) | copy-start | bytes 13828
  83.1 10.5 %all-to-all-start.4 = ((bf16[128,4,288]{0,2,1:T(8,128)(2,1)}), bf16[128,4,288]{0,2,1:T(8,128)(2,1)}, u32[]{:S(2)}, u32[]{:S(2)}) async-start(bf16[128,4,288]{0,2,1:T(8,128)(2,1)} %copy.108), calls=%async_computation.4 | async-start | bytes 589824 | tf_op jit(solution)/shard_map/all_to_all | solution.py:79
  87.2 120.0 %reduce-scatter.2.cloned.1.call-start = ((), (), s32[]{:S(2)}) async-start(), calls=%async_computation.6 | async-start | bytes 3981312 | tf_op jit(solution)/shard_map/reduce_scatter | solution.py:110
  127.6 0.9 copy-start.4
  127.6 2.0 copy-start.7
  129.5 2.7 %copy-start.11 = (f32[32,16,4]{2,1,0:T(8,128)}, f32[32,16,4]{2,1,0:T(8,128)S(1)}, u32[]{:S(2)}) copy-start(f32[32,16,4]{2,1,0:T(8,128)S(1)} %negate_divide_fusion) | copy-start | bytes 24580
Sparse Core Ops, SparseCore 0:
  9.5 25.8 all-gather.2
  127.7 79.3 reduce-scatter.1
